TPU v7x, 512 devices: a whole 4x4x16 slice. The times are simulated.
512 devices in a mesh: lon: 32 (over x, z_lo), lat: 16 (over y, z_hi, core).
Axes of the slice: x: 4, y: 4, z: 16 (z_hi: 2, z_lo: 8; z = z_hi * 8 + z_lo), core: 2. Of those that a mesh axis runs over, the one named last changes fastest.
Arguments:
- increment: bfloat16 [2, 127, 128, 4096], P(None, None, 'lat', 'lon'), may hold values from -6 to 6
- std_dev: bfloat16 [2, 127, 128, 4096], P(None, None, 'lat', 'lon'), may hold values from 0.5 to 4
- level_group: int32 [127], replicated, may hold values from 0 to 3, never falling along the last dimension, each value on 1 to 40 neighbouring positions
- lon_reach: float32 [2, 4, 4], replicated, may hold values from 8 to 16384
- lon_weight: float32 [2, 4, 4], replicated, may hold values from 0.2 to 1
- lat_reach: float32 [2, 4, 4], replicated, may hold values from 2 to 512
- lat_weight: float32 [2, 4, 4], replicated, may hold values from 0.2 to 1
- vertical: float32 [2, 127, 127], replicated, may hold values from -0.5 to 0.5
Outputs:
- covaried: bfloat16 [2, 127, 128, 4096], P(None, None, 'lat', 'lon')
Inputs may be any that keep to these rules, and one draw needn't show every extreme that they name: level_group never falls along the levels; each of the 4 groups holds 1 to 40 consecutive levels and one holds exactly 40.
All inputs are finite; a program needn't handle non-finite values.
Results may differ from a plain program's by a relative error of at most 0.003.
Values sent between devices are 32-bit elements; how exact they have to be, the bound alone decides.
A program may use at most 64 MiB of HBM per device.

v0:
```python
import jax
import jax.numpy as jnp
from jax import lax
from jax.sharding import PartitionSpec as P

MOST = 40


def prefix_2(part, axis, combine, identity, reverse):
    count = lax.axis_size(axis)
    place = lax.axis_index(axis)
    ahead = count - 1 - place if reverse else place
    gathered = jax.tree.map(lambda a: lax.all_gather(a, axis), part)
    state = jax.tree.map(lambda a, e: jnp.zeros_like(a) + jnp.asarray(e, a.dtype), part, identity)

    def one(step, state):
        source = count - 1 - step if reverse else step
        return combine(
            state, jax.tree.map(lambda a: lax.dynamic_index_in_dim(a, source, 0, False), gathered)
        )

    return lax.fori_loop(0, ahead, one, state)


def from_root(value, axis, source):
    kept = jnp.where(lax.axis_index(axis) == source, value, 0).astype(value.dtype)
    return lax.psum(kept, axis)


def level_values(onehot, grouped):
    return jnp.einsum("kg,vgp->vkp", onehot, grouped, precision=lax.Precision.HIGHEST)


def toeplitz_tables(inverse_group, weights_group, length):
    indices = jnp.arange(length)
    spacing = (indices[None, :] - indices[:, None]).astype(jnp.float32)
    rates = jnp.exp(-jnp.maximum(spacing, 0.0) * inverse_group[..., None, None])
    terms = jnp.sum(weights_group[..., None, None] * rates, axis=2)
    return jnp.where(spacing >= 0.0, terms, 0.0)


def grouped_product(current, blocks, level_group, pattern):
    levels = current.shape[1]
    result = jnp.zeros_like(current)
    for group in range(blocks.shape[1]):
        first_level = jnp.minimum(jnp.sum((level_group < group).astype(jnp.int32)), levels - MOST)
        window = lax.dynamic_slice_in_dim(current, first_level, MOST, 1)
        product = jnp.einsum(pattern, window, blocks[:, group], precision=lax.Precision.HIGHEST)
        labels = lax.dynamic_slice_in_dim(level_group, first_level, MOST, 0)
        member_mask = (labels == group)[None, :, None, None]
        previous = lax.dynamic_slice_in_dim(result, first_level, MOST, 1)
        result = lax.dynamic_update_slice_in_dim(
            result, previous + jnp.where(member_mask, product, 0.0), first_level, 1
        )
    return result


def affine_join(earlier, later):
    return (earlier[0] * later[0], later[0] * earlier[1] + later[1])


def cycle_carry(edge_sums, inverse_level, length, reverse):
    members = lax.axis_size("lon")
    inverse = jnp.transpose(inverse_level, (2, 0, 1))[..., None]
    closure = 1.0 - jnp.exp(-(members * length) * inverse)
    stride = jnp.exp(-length * inverse)
    factor, prefix = prefix_2(
        (stride, edge_sums),
        "lon",
        affine_join,
        (jnp.ones_like(stride), jnp.zeros_like(edge_sums)),
        reverse,
    )
    leaving = stride * prefix + edge_sums
    anchor = 0 if reverse else members - 1
    beside_all = from_root(leaving, "lon", anchor)
    return prefix + factor * beside_all / closure


def band_carry(edge_sums, inverse_level, length, reverse):
    inverse = jnp.transpose(inverse_level, (2, 0, 1))[..., None]
    stride = jnp.exp(-length * inverse)
    factor, prefix = prefix_2(
        (stride, edge_sums),
        "lat",
        affine_join,
        (jnp.ones_like(stride), jnp.zeros_like(edge_sums)),
        reverse,
    )
    return prefix


def lon_pass(current, blocks, inverse, weights, level_group, reverse):
    cells = current.shape[3]
    position = jnp.arange(cells).astype(jnp.float32)
    if reverse:
        edge_gap = position
        inward = cells - position
        pattern = "vkaj,vij->vkai"
    else:
        edge_gap = cells - 1.0 - position
        inward = position + 1.0
        pattern = "vkaj,vji->vkai"
    edge_weight = jnp.exp(-edge_gap * inverse[..., None])
    edge_sums = jnp.einsum("vkal,vkpl->pvka", current, edge_weight, precision=lax.Precision.HIGHEST)
    inside = grouped_product(current, blocks, level_group, pattern)
    incoming = cycle_carry(edge_sums, inverse, cells, reverse)
    decay = weights[..., None] * jnp.exp(-inward * inverse[..., None])
    return inside + jnp.einsum("pvka,vkpl->vkal", incoming, decay, precision=lax.Precision.HIGHEST)


def lat_pass(current, blocks, inverse, weights, level_group, reverse):
    height = current.shape[2]
    position = jnp.arange(height).astype(jnp.float32)
    if reverse:
        edge_gap = position
        inward = height - position
        pattern = "vkjl,vij->vkil"
    else:
        edge_gap = height - 1.0 - position
        inward = position + 1.0
        pattern = "vkjl,vji->vkil"
    edge_weight = jnp.exp(-edge_gap * inverse[..., None])
    edge_sums = jnp.einsum("vkal,vkpa->pvkl", current, edge_weight, precision=lax.Precision.HIGHEST)
    inside = grouped_product(current, blocks, level_group, pattern)
    incoming = band_carry(edge_sums, inverse, height, reverse)
    decay = weights[..., None] * jnp.exp(-inward * inverse[..., None])
    return inside + jnp.einsum("pvkl,vkpa->vkal", incoming, decay, precision=lax.Precision.HIGHEST)


def per_device(
    increment, std_dev, level_group, lon_reach, lon_weight, lat_reach, lat_weight, vertical
):
    height = increment.shape[2]
    cells = increment.shape[3]
    groups = lon_reach.shape[1]
    onehot = (level_group[:, None] == jnp.arange(groups, dtype=jnp.int32)[None, :]).astype(
        jnp.float32
    )
    inverse_lon_group = 1.0 / lon_reach
    weights_lon_group = lon_weight * (1.0 - jnp.exp(-inverse_lon_group))
    inverse_lat_group = 1.0 / lat_reach
    weights_lat_group = lat_weight * (1.0 - jnp.exp(-inverse_lat_group))
    inverse_lon = level_values(onehot, inverse_lon_group)
    inverse_lat = level_values(onehot, inverse_lat_group)
    weights_lat = level_values(onehot, weights_lat_group)
    blocks_lat = toeplitz_tables(inverse_lat_group, weights_lat_group, height)
    spread_dev = std_dev.astype(jnp.float32)
    current = spread_dev * increment.astype(jnp.float32)
    weights_lon = level_values(onehot, weights_lon_group)
    blocks_lon = toeplitz_tables(inverse_lon_group, weights_lon_group, cells)
    current = lon_pass(current, blocks_lon, inverse_lon, weights_lon, level_group, False)
    current = lon_pass(current, blocks_lon, inverse_lon, weights_lon, level_group, True)
    current = lat_pass(current, blocks_lat, inverse_lat, weights_lat, level_group, False)
    current = lat_pass(current, blocks_lat, inverse_lat, weights_lat, level_group, True)
    mixed = jnp.einsum("vkj,vjal->vkal", vertical, current, precision=lax.Precision.HIGHEST)
    return (spread_dev * mixed).astype(jnp.bfloat16)


def solution(mesh):
    placed = (
        P(None, None, "lat", "lon"),
        P(None, None, "lat", "lon"),
        P(),
        P(),
        P(),
        P(),
        P(),
        P(),
    )
    return jax.shard_map(
        per_device,
        mesh=mesh,
        in_specs=placed,
        out_specs=P(None, None, "lat", "lon"),
        check_vma=False,
    )
```

profile of v0, /device:TPU:2, one launch (start us, length us, event | category | flops | bytes accessed | tf_op | source)
XLA Modules:
  0.0 1333.2 jit_solution(13357171241874565079)
XLA Ops:
  6.5 1.5 fusion.120
  13.5 0.7 subtract_multiply_fusion
  14.2 0.8 fusion.125
  15.0 1.5 convolution_bitcast_fusion.5
  16.5 1.4 multiply_reduce_fusion
  18.6 1.4 convert_multiply_fusion.1
  20.0 1.9 convolution_bitcast_fusion.3
  22.1 122.4 %all-gather.1 = f32[128,2,127,8]{2,3,1,0:T(8,128)S(1)} all-gather(f32[4,2,127,8]{2,3,1,0:T(8,128)S(1)} %copy.93), channel_id=3, replica_groups=mesh['lon'=32,'lat'=16] {'lon'}, dimensions={0}, use_global_device_ids=true | all-gather | bytes 1072896 | tf_op jit(solution)/shard_map/all_gather | solution.py:13
  144.5 102.7 %all-gather = f32[128,2,127]{2,1,0:T(2,128)S(1)} all-gather(f32[4,2,127]{2,1,0:T(2,128)S(1)} %copy.91), channel_id=2, replica_groups=mesh['lon'=32,'lat'=16] {'lon'}, dimensions={0}, use_global_device_ids=true | all-gather | bytes 134112 | tf_op jit(solution)/shard_map/all_gather | solution.py:13
  247.2 0.8 while.52
  248.7 226.5 %psum.14 = f32[4,2,127,8]{3,0,2,1:T(4,128)S(1)} all-reduce(f32[4,2,127,8]{3,0,2,1:T(4,128)S(1)} %add_select_fusion.1), channel_id=1, replica_groups=mesh['lon'=32,'lat'=16] {'lon'}, use_global_device_ids=true, to_apply=%region_8.9 | all-reduce | flops 8128 | bytes 65024 | tf_op jit(solution)/shard_map/psum | solution.py:27
  475.3 0.8 copy.100
  477.3 0.8 copy.103
  478.1 0.8 copy_select_fusion
  481.0 2.8 convolution_add_fusion.3
  483.8 1.0 copy-done.2
  484.8 1.9 convolution_bitcast_fusion.2
  486.9 119.1 %all-gather.2 = f32[128,2,127,8]{2,3,1,0:T(8,128)S(1)} all-gather(f32[4,2,127,8]{2,3,1,0:T(8,128)S(1)} %copy.105), channel_id=4, replica_groups=mesh['lon'=32,'lat'=16] {'lon'}, dimensions={0}, use_global_device_ids=true | all-gather | bytes 1072896 | tf_op jit(solution)/shard_map/all_gather | solution.py:13
  606.0 32.0 %while.53 = (s32[]{:T(128)}, f32[4,2,127,1]{2,3,1,0:T(1,128)S(1)}, f32[4,2,127,8]{2,3,1,0:T(8,128)S(1)}, s32[]{:T(128)}, f32[32,4,2,127,1]{3,2,1,4,0:T(2,128)}, ...) while((s32[]{:T(128)}, f32[4,2,127,1]{2,3,1,0:T(1,128)S(1)}, ...), condition=%wide.region_10.11_spmd, body=%wide.region_9.10_spmd.sunk | while | flops 17278 | bytes 130207 | solution.py:22
  608.1 0.7 constant_dynamic-slice_fusion.9
  610.8 0.7 constant_dynamic-slice_fusion.9
  615.0 0.7 constant_dynamic-slice_fusion.9
  619.2 0.7 constant_dynamic-slice_fusion.9
  621.2 0.7 fusion.143
  621.9 0.7 constant_dynamic-slice_fusion.9
  623.3 0.7 constant_dynamic-slice_fusion.9
  626.1 0.7 constant_dynamic-slice_fusion.9
  630.3 0.7 constant_dynamic-slice_fusion.9
  633.1 0.7 constant_dynamic-slice_fusion.9
  637.2 0.7 constant_dynamic-slice_fusion.9
  638.4 245.2 %psum.15 = f32[4,2,127,8]{3,0,2,1:T(4,128)S(1)} all-reduce(f32[4,2,127,8]{3,0,2,1:T(4,128)S(1)} %add_select_fusion), channel_id=1, replica_groups=mesh['lon'=32,'lat'=16] {'lon'}, use_global_device_ids=true, to_apply=%region_11.12 | all-reduce | flops 8128 | bytes 65024 | tf_op jit(solution)/shard_map/psum | solution.py:27
  884.6 1.0 copy.112
  885.7 1.4 fusion.24
  887.1 1.4 fusion.33
  890.0 3.9 convolution_add_fusion.2
  894.0 1.9 convolution_bitcast_fusion.1
  895.9 1.1 copy.122
  897.2 0.8 copy.118
  898.1 42.6 %all-gather.3 = f32[64,2,127]{2,1,0:T(2,128)S(1)} all-gather(f32[4,2,127]{2,1,0:T(2,128)S(1)} %copy.121), channel_id=5, replica_groups=mesh['lon'=32,'lat'=16] {'lat'}, dimensions={0}, use_global_device_ids=true | all-gather | bytes 69088 | tf_op jit(solution)/shard_map/all_gather | solution.py:13
  942.9 159.9 %all-gather.9.cloned.1.call-done = f32[64,2,127,128]{3,1,2,0:T(2,128)} async-done(((f32[4,2,127,128]{3,1,2,0:T(2,128)}), f32[64,2,127,128]{3,1,2,0:T(2,128)}) %all-gather.9.cloned.1.call-update) | async-done | bytes 8323088 | tf_op jit(solution)/shard_map/all_gather | solution.py:13
  1103.1 0.7 copy-done.10
  1103.8 4.0 convolution_add_fusion.1
  1107.7 1.9 convolution_bitcast_fusion
  1109.7 1.1 copy.126
  1112.6 186.0 %all-gather.11.cloned.1.call-done = f32[64,2,127,128]{3,1,2,0:T(2,128)} async-done(((f32[4,2,127,128]{3,1,2,0:T(2,128)}), f32[64,2,127,128]{3,1,2,0:T(2,128)}) %all-gather.11.cloned.1.call-update) | async-done | bytes 8323088 | tf_op jit(solution)/shard_map/all_gather | solution.py:13
  1298.6 21.4 %while.55 = (s32[]{:T(128)}, f32[4,2,127,128]{3,2,1,0:T(8,128)S(1)}, s32[]{:T(128)}, f32[16,4,2,127,1]{3,2,1,4,0:T(2,128)S(1)}, f32[16,4,2,127,128]{4,2,3,1,0:T(...) while((s32[]{:T(128)}, f32[4,2,127,128]{3,2,1,0:T(8,128)S(1)}, s32[]{:T(128)}, ...), condition=%wide.region_15.16_spmd, body=%wide.region_14.15_spmd.sunk | while | flops 260102 | bytes 2613299 | solution.py:22
  1298.6 1.1 constant_dynamic-slice_fusion.11
  1300.1 1.1 constant_dynamic-slice_fusion.11
  1301.5 1.1 constant_dynamic-slice_fusion.11
  1302.9 1.1 constant_dynamic-slice_fusion.11
  1304.3 1.1 constant_dynamic-slice_fusion.11
  1305.7 1.1 constant_dynamic-slice_fusion.11
  1307.1 1.1 constant_dynamic-slice_fusion.11
  1308.5 1.1 constant_dynamic-slice_fusion.11
  1309.9 1.1 constant_dynamic-slice_fusion.11
  1311.3 1.1 constant_dynamic-slice_fusion.11
  1312.7 1.1 constant_dynamic-slice_fusion.11
  1314.1 1.1 constant_dynamic-slice_fusion.11
  1315.5 1.1 constant_dynamic-slice_fusion.11
  1317.0 1.1 constant_dynamic-slice_fusion.11
  1318.4 1.1 constant_dynamic-slice_fusion.11
  1320.0 3.0 convolution_add_fusion
  1323.0 1.8 fusion.38
  1325.3 0.9 fusion.40
  (268 shorter events, 44.6 us)
Async XLA Ops:
  6.5 1316.4 %copy-start = (f32[2,127,127]{2,0,1:T(2,128)S(1)}, f32[2,127,127]{2,0,1:T(2,128)}, u32[]{:S(2)}) copy-start(f32[2,127,127]{2,0,1:T(2,128)} %param.23) | copy-start | bytes 387100
  6.5 13.4 %copy-start.5 = (bf16[2,127,8,128]{3,2,1,0:T(8,128)(2,1)S(1)}, bf16[2,127,8,128]{3,2,1,0:T(8,128)(2,1)}, u32[]{:S(2)}) copy-start(bf16[2,127,8,128]{3,2,1,0:T(8,128)(2,1)} %param.16) | copy-start | bytes 1560580
  6.5 13.4 %copy-start.1 = (bf16[2,127,8,128]{3,2,1,0:T(8,128)(2,1)S(1)}, bf16[2,127,8,128]{3,2,1,0:T(8,128)(2,1)}, u32[]{:S(2)}) copy-start(bf16[2,127,8,128]{3,2,1,0:T(8,128)(2,1)} %param.17) | copy-start | bytes 1560580
  6.5 1096.3 %all-gather.9.cloned.1.call-start = ((), (), s32[]{:S(2)}) async-start(), calls=%async_computation | async-start | bytes 8843264 | tf_op jit(solution)/shard_map/all_gather | solution.py:13
  18.6 1.4 copy-start.7
  144.5 330.6 %copy-start.13 = (f32[4,2,127]{2,1,0:T(2,128)}, f32[4,2,127]{2,1,0:T(2,128)S(1)}, u32[]{:S(2)}) copy-start(f32[4,2,127]{2,1,0:T(2,128)S(1)} %copy.91) | copy-start | bytes 12196
  248.0 0.6 copy-start.6
  475.2 3.0 copy-start.4
  475.2 3.8 copy-start.15
  478.1 2.9 copy-start.12
  479.0 406.6 %copy-start.20 = (pred[40]{0:T(512)(128)(4,1)}, pred[40]{0:T(512)(128)(4,1)S(1)}, u32[]{:S(2)}) copy-start(pred[40]{0:T(512)(128)(4,1)S(1)} %get-tuple-element.377) | copy-start | bytes 124
  479.0 408.1 %copy-start.18 = (pred[40]{0:T(512)(128)(4,1)}, pred[40]{0:T(512)(128)(4,1)S(1)}, u32[]{:S(2)}) copy-start(pred[40]{0:T(512)(128)(4,1)S(1)} %get-tuple-element.376) | copy-start | bytes 124
  479.1 409.6 %copy-start.16 = (pred[40]{0:T(512)(128)(4,1)}, pred[40]{0:T(512)(128)(4,1)S(1)}, u32[]{:S(2)}) copy-start(pred[40]{0:T(512)(128)(4,1)S(1)} %get-tuple-element.375) | copy-start | bytes 124
  479.1 1.8 copy-start.8
  479.2 1.8 copy-start.27
  481.0 3.8 copy-start.26
  483.8 1.0 copy-start.2
  484.8 153.1 %copy-start.14 = (f32[4,2,127]{2,1,0:T(2,128)S(1)}, f32[4,2,127]{2,1,0:T(2,128)}, u32[]{:S(2)}) copy-start(f32[4,2,127]{2,1,0:T(2,128)} %copy-done.13) | copy-start | bytes 12196
  884.6 4.1 copy-start.3
  885.7 3.9 copy-start.22
  885.7 3.9 copy-start.23
  885.7 4.3 copy-start.25
  889.6 4.3 copy-start.24
  890.0 5.9 copy-start.9
  893.9 47.0 %copy-start.21 = (pred[40]{0:T(512)(128)(4,1)S(1)}, pred[40]{0:T(512)(128)(4,1)}, u32[]{:S(2)}) copy-start(pred[40]{0:T(512)(128)(4,1)} %copy-done.20) | copy-start | bytes 124
  895.9 45.5 %copy-start.19 = (pred[40]{0:T(512)(128)(4,1)S(1)}, pred[40]{0:T(512)(128)(4,1)}, u32[]{:S(2)}) copy-start(pred[40]{0:T(512)(128)(4,1)} %copy-done.18) | copy-start | bytes 124
  895.9 46.0 %copy-start.17 = (pred[40]{0:T(512)(128)(4,1)S(1)}, pred[40]{0:T(512)(128)(4,1)}, u32[]{:S(2)}) copy-start(pred[40]{0:T(512)(128)(4,1)} %copy-done.16) | copy-start | bytes 124
  897.0 401.6 %all-gather.11.cloned.1.call-start = ((), (), s32[]{:S(2)}) async-start(), calls=%async_computation.1 | async-start | bytes 8843264 | tf_op jit(solution)/shard_map/all_gather | solution.py:13
  1102.9 0.9 copy-start.10
  1298.6 21.4 %copy-start.11 = (f32[2,127,4]{2,1,0:T(8,128)S(1)}, f32[2,127,4]{2,1,0:T(8,128)}, u32[]{:S(2)}) copy-start(f32[2,127,4]{2,1,0:T(8,128)} %copy.118) | copy-start | bytes 12196
Sparse Core Ops, SparseCore 0:
  897.1 205.6 all-gather.8
  1110.9 187.6 all-gather.10
where the time goes:
time: 1340 us; the launch traced here: 1330 us
  blocking collectives  858 us (64%)
  waiting for transfers between devices  346 us (26%)
  local copies, waits for them, and re-layouts  58.4 us (4%)
  matrix products  35.1 us (3%)
  between operations  17 us (1%)
  other arithmetic  16.9 us (1%)
    psum x2, blocking collectives, from_root(): return lax.psum(kept, axis)  472 us
    all_gather x4, blocking collectives, prefix_2(): gathered = jax.tree.map(lambda a: lax.all_gather(a, axis), part)  387 us
    all_gather x2, waiting for transfers between devices, prefix_2(): gathered = jax.tree.map(lambda a: lax.all_gather(a, axis), part)  346 us
    dynamic_slice x46, local copies, waits for them, and re-layouts, one(): lax.dynamic_index_in_dim(a, source, 0, False)  32 us
  transfers between devices with their start and end apart: 2, of which 2 were waited for; matrix products, arithmetic and copies ran while one was open for 0% of the time, Pallas kernels for 0%

commit v1 on v0

--- a/solution.py
+++ b/solution.py
@@ -24,7 +24,8 @@
 
 def from_root(value, axis, source):
     kept = jnp.where(lax.axis_index(axis) == source, value, 0).astype(value.dtype)
-    return lax.psum(kept, axis)
+    row_match = lambda z_in, which_axis: lax.all_gather(z_in, which_axis).sum(axis=0)
+    return row_match(kept, axis)
 
 
 def level_values(onehot, grouped):

time: 1340 us -> 1120 us (0.84)
  blocking collectives: 858 us -> 638 us
    psum x2 -> x0, blocking collectives: 472 us -> none  [from_root(): return lax.psum(kept, axis)]
    all_gather x0 -> x2, blocking collectives: none -> 250 us  [from_root(): lax.all_gather(z_in, which_axis).sum(axis=0)]
where the time goes in v1:
time: 1120 us; the launch traced here: 1110 us
  blocking collectives  638 us (57%)
  waiting for transfers between devices  344 us (31%)
  local copies, waits for them, and re-layouts  59.1 us (5%)
  matrix products  35.1 us (3%)
  other arithmetic  17.1 us (2%)
  between operations  16.9 us (2%)
    all_gather x4, blocking collectives, prefix_2(): gathered = jax.tree.map(lambda a: lax.all_gather(a, axis), part)  388 us
    all_gather x2, waiting for transfers between devices, prefix_2(): gathered = jax.tree.map(lambda a: lax.all_gather(a, axis), part)  344 us
    all_gather x2, blocking collectives, from_root(): lax.all_gather(z_in, which_axis).sum(axis=0)  250 us
    dynamic_slice x46, local copies, waits for them, and re-layouts, one(): lax.dynamic_index_in_dim(a, source, 0, False)  32 us
  transfers between devices with their start and end apart: 2, of which 2 were waited for; matrix products, arithmetic and copies ran while one was open for 0% of the time, Pallas kernels for 0%

profile of v1, /device:TPU:2, one launch (start us, length us, event | category | flops | bytes accessed | tf_op | source)
XLA Modules:
  0.0 1111.8 jit_solution(6695777908733800528)
XLA Ops:
  6.5 1.5 fusion.120
  13.5 0.7 subtract_multiply_fusion
  14.2 0.8 fusion.125
  15.0 1.5 convolution_bitcast_fusion.5
  16.5 1.4 multiply_reduce_fusion
  18.6 1.4 convert_multiply_fusion.1
  20.0 1.9 convolution_bitcast_fusion.3
  22.1 122.4 %all-gather.1 = f32[128,2,127,8]{2,3,1,0:T(8,128)S(1)} all-gather(f32[4,2,127,8]{2,3,1,0:T(8,128)S(1)} %copy.93), channel_id=3, replica_groups=mesh['lon'=32,'lat'=16] {'lon'}, dimensions={0}, use_global_device_ids=true | all-gather | bytes 1072896 | tf_op jit(solution)/shard_map/all_gather | solution.py:13
  144.5 102.6 %all-gather = f32[128,2,127]{2,1,0:T(2,128)S(1)} all-gather(f32[4,2,127]{2,1,0:T(2,128)S(1)} %copy.91), channel_id=2, replica_groups=mesh['lon'=32,'lat'=16] {'lon'}, dimensions={0}, use_global_device_ids=true | all-gather | bytes 134112 | tf_op jit(solution)/shard_map/all_gather | solution.py:13
  247.1 0.8 while.52
  248.6 114.7 %all-gather.2 = f32[128,2,127,8]{2,3,1,0:T(8,128)S(1)} all-gather(f32[4,2,127,8]{2,3,1,0:T(8,128)S(1)} %copy.100), channel_id=4, replica_groups=mesh['lon'=32,'lat'=16] {'lon'}, dimensions={0}, use_global_device_ids=true | all-gather | bytes 1072896 | tf_op jit(solution)/shard_map/all_gather | solution.py:27
  363.8 0.8 copy.102
  365.7 0.8 copy.105
  366.6 0.8 copy_select_fusion
  369.4 2.8 convolution_add_fusion.3
  372.3 1.0 copy-done.2
  373.2 1.9 convolution_bitcast_fusion.2
  375.3 120.9 %all-gather.3 = f32[128,2,127,8]{2,3,1,0:T(8,128)S(1)} all-gather(f32[4,2,127,8]{2,3,1,0:T(8,128)S(1)} %copy.107), channel_id=5, replica_groups=mesh['lon'=32,'lat'=16] {'lon'}, dimensions={0}, use_global_device_ids=true | all-gather | bytes 1072896 | tf_op jit(solution)/shard_map/all_gather | solution.py:13
  496.2 32.0 %while.53 = (s32[]{:T(128)}, f32[4,2,127,1]{2,3,1,0:T(1,128)S(1)}, f32[4,2,127,8]{2,3,1,0:T(8,128)S(1)}, s32[]{:T(128)}, f32[32,4,2,127,1]{3,2,1,4,0:T(2,128)}, ...) while((s32[]{:T(128)}, f32[4,2,127,1]{2,3,1,0:T(1,128)S(1)}, ...), condition=%wide.region_10.11_spmd, body=%wide.region_9.10_spmd.sunk | while | flops 17278 | bytes 130207 | solution.py:22
  498.3 0.7 constant_dynamic-slice_fusion.9
  501.1 0.7 constant_dynamic-slice_fusion.9
  505.3 0.7 constant_dynamic-slice_fusion.9
  509.4 0.7 constant_dynamic-slice_fusion.9
  511.5 0.7 fusion.143
  512.2 0.7 constant_dynamic-slice_fusion.9
  513.6 0.7 constant_dynamic-slice_fusion.9
  516.4 0.7 constant_dynamic-slice_fusion.9
  520.6 0.7 constant_dynamic-slice_fusion.9
  523.4 0.7 constant_dynamic-slice_fusion.9
  527.5 0.7 constant_dynamic-slice_fusion.9
  528.9 135.1 %all-gather.4 = f32[128,2,127,8]{2,3,1,0:T(8,128)S(1)} all-gather(f32[4,2,127,8]{2,3,1,0:T(8,128)S(1)} %copy.113), channel_id=6, replica_groups=mesh['lon'=32,'lat'=16] {'lon'}, dimensions={0}, use_global_device_ids=true | all-gather | bytes 1072896 | tf_op jit(solution)/shard_map/all_gather | solution.py:27
  665.3 1.0 copy.116
  666.4 1.4 fusion.24
  667.9 1.5 fusion.33
  670.7 3.9 convolution_add_fusion.2
  674.7 1.9 convolution_bitcast_fusion.1
  676.6 1.1 copy.126
  678.0 0.8 copy.122
  678.8 42.1 %all-gather.5 = f32[64,2,127]{2,1,0:T(2,128)S(1)} all-gather(f32[4,2,127]{2,1,0:T(2,128)S(1)} %copy.125), channel_id=7, replica_groups=mesh['lon'=32,'lat'=16] {'lat'}, dimensions={0}, use_global_device_ids=true | all-gather | bytes 69088 | tf_op jit(solution)/shard_map/all_gather | solution.py:13
  723.1 158.2 %all-gather.11.cloned.1.call-done = f32[64,2,127,128]{3,1,2,0:T(2,128)} async-done(((f32[4,2,127,128]{3,1,2,0:T(2,128)}), f32[64,2,127,128]{3,1,2,0:T(2,128)}) %all-gather.11.cloned.1.call-update) | async-done | bytes 8323088 | tf_op jit(solution)/shard_map/all_gather | solution.py:13
  881.6 0.7 copy-done.10
  882.3 4.0 convolution_add_fusion.1
  886.3 1.9 convolution_bitcast_fusion
  888.2 1.1 copy.130
  891.1 186.0 %all-gather.13.cloned.1.call-done = f32[64,2,127,128]{3,1,2,0:T(2,128)} async-done(((f32[4,2,127,128]{3,1,2,0:T(2,128)}), f32[64,2,127,128]{3,1,2,0:T(2,128)}) %all-gather.13.cloned.1.call-update) | async-done | bytes 8323088 | tf_op jit(solution)/shard_map/all_gather | solution.py:13
  1077.1 21.4 %while.55 = (s32[]{:T(128)}, f32[4,2,127,128]{3,2,1,0:T(8,128)S(1)}, s32[]{:T(128)}, f32[16,4,2,127,1]{3,2,1,4,0:T(2,128)S(1)}, f32[16,4,2,127,128]{4,2,3,1,0:T(...) while((s32[]{:T(128)}, f32[4,2,127,128]{3,2,1,0:T(8,128)S(1)}, s32[]{:T(128)}, ...), condition=%wide.region_15.16_spmd, body=%wide.region_14.15_spmd.sunk | while | flops 260102 | bytes 2613299 | solution.py:22
  1077.2 1.1 constant_dynamic-slice_fusion.11
  1078.6 1.1 constant_dynamic-slice_fusion.11
  1080.0 1.1 constant_dynamic-slice_fusion.11
  1081.4 1.1 constant_dynamic-slice_fusion.11
  1082.8 1.1 constant_dynamic-slice_fusion.11
  1084.2 1.1 constant_dynamic-slice_fusion.11
  1085.6 1.1 constant_dynamic-slice_fusion.11
  1087.0 1.1 constant_dynamic-slice_fusion.11
  1088.4 1.1 constant_dynamic-slice_fusion.11
  1089.9 1.1 constant_dynamic-slice_fusion.11
  1091.3 1.1 constant_dynamic-slice_fusion.11
  1092.7 1.1 constant_dynamic-slice_fusion.11
  1094.1 1.1 constant_dynamic-slice_fusion.11
  1095.5 1.1 constant_dynamic-slice_fusion.11
  1096.9 1.1 constant_dynamic-slice_fusion.11
  1098.5 3.0 convolution_add_fusion
  1101.5 1.8 fusion.38
  1103.8 0.9 fusion.40
  (274 shorter events, 45.5 us)
Async XLA Ops:
  6.5 1095.0 %copy-start = (f32[2,127,127]{2,0,1:T(2,128)S(1)}, f32[2,127,127]{2,0,1:T(2,128)}, u32[]{:S(2)}) copy-start(f32[2,127,127]{2,0,1:T(2,128)} %param.23) | copy-start | bytes 387100
  6.5 13.4 %copy-start.5 = (bf16[2,127,8,128]{3,2,1,0:T(8,128)(2,1)S(1)}, bf16[2,127,8,128]{3,2,1,0:T(8,128)(2,1)}, u32[]{:S(2)}) copy-start(bf16[2,127,8,128]{3,2,1,0:T(8,128)(2,1)} %param.16) | copy-start | bytes 1560580
  6.5 13.4 %copy-start.1 = (bf16[2,127,8,128]{3,2,1,0:T(8,128)(2,1)S(1)}, bf16[2,127,8,128]{3,2,1,0:T(8,128)(2,1)}, u32[]{:S(2)}) copy-start(bf16[2,127,8,128]{3,2,1,0:T(8,128)(2,1)} %param.17) | copy-start | bytes 1560580
  6.5 874.8 %all-gather.11.cloned.1.call-start = ((), (), s32[]{:S(2)}) async-start(), calls=%async_computation | async-start | bytes 8843264 | tf_op jit(solution)/shard_map/all_gather | solution.py:13
  18.6 1.4 copy-start.7
  144.5 218.7 %copy-start.13 = (f32[4,2,127]{2,1,0:T(2,128)}, f32[4,2,127]{2,1,0:T(2,128)S(1)}, u32[]{:S(2)}) copy-start(f32[4,2,127]{2,1,0:T(2,128)S(1)} %copy.91) | copy-start | bytes 12196
  247.9 115.4 %copy-start.6 = (f32[32,4,2,127,1]{3,2,1,4,0:T(2,128)}, f32[32,4,2,127,1]{3,2,1,4,0:T(2,128)S(1)}, u32[]{:S(2)}) copy-start(f32[32,4,2,127,1]{3,2,1,4,0:T(2,128)S(1)} %get-tuple-element.634) | copy-start | bytes 390148
  363.3 3.3 copy-start.4
  363.6 3.8 copy-start.15
  366.5 2.9 copy-start.12
  367.5 298.9 %copy-start.20 = (pred[40]{0:T(512)(128)(4,1)}, pred[40]{0:T(512)(128)(4,1)S(1)}, u32[]{:S(2)}) copy-start(pred[40]{0:T(512)(128)(4,1)S(1)} %get-tuple-element.377) | copy-start | bytes 124
  367.5 300.4 %copy-start.18 = (pred[40]{0:T(512)(128)(4,1)}, pred[40]{0:T(512)(128)(4,1)S(1)}, u32[]{:S(2)}) copy-start(pred[40]{0:T(512)(128)(4,1)S(1)} %get-tuple-element.376) | copy-start | bytes 124
  367.5 301.8 %copy-start.16 = (pred[40]{0:T(512)(128)(4,1)}, pred[40]{0:T(512)(128)(4,1)S(1)}, u32[]{:S(2)}) copy-start(pred[40]{0:T(512)(128)(4,1)S(1)} %get-tuple-element.375) | copy-start | bytes 124
  367.6 1.8 copy-start.8
  367.6 1.8 copy-start.27
  369.4 3.8 copy-start.26
  372.3 1.0 copy-start.2
  373.2 155.0 %copy-start.14 = (f32[4,2,127]{2,1,0:T(2,128)S(1)}, f32[4,2,127]{2,1,0:T(2,128)}, u32[]{:S(2)}) copy-start(f32[4,2,127]{2,1,0:T(2,128)} %copy-done.13) | copy-start | bytes 12196
  665.3 4.1 copy-start.3
  666.4 3.9 copy-start.22
  666.4 3.9 copy-start.23
  666.4 4.3 copy-start.25
  670.3 4.4 copy-start.24
  670.7 5.9 copy-start.9
  674.7 46.4 %copy-start.21 = (pred[40]{0:T(512)(128)(4,1)S(1)}, pred[40]{0:T(512)(128)(4,1)}, u32[]{:S(2)}) copy-start(pred[40]{0:T(512)(128)(4,1)} %copy-done.20) | copy-start | bytes 124
  676.6 45.0 %copy-start.19 = (pred[40]{0:T(512)(128)(4,1)S(1)}, pred[40]{0:T(512)(128)(4,1)}, u32[]{:S(2)}) copy-start(pred[40]{0:T(512)(128)(4,1)} %copy-done.18) | copy-start | bytes 124
  676.6 45.5 %copy-start.17 = (pred[40]{0:T(512)(128)(4,1)S(1)}, pred[40]{0:T(512)(128)(4,1)}, u32[]{:S(2)}) copy-start(pred[40]{0:T(512)(128)(4,1)} %copy-done.16) | copy-start | bytes 124
  677.7 399.4 %all-gather.13.cloned.1.call-start = ((), (), s32[]{:S(2)}) async-start(), calls=%async_computation.1 | async-start | bytes 8843264 | tf_op jit(solution)/shard_map/all_gather | solution.py:13
  881.4 0.9 copy-start.10
  1077.1 21.4 %copy-start.11 = (f32[2,127,4]{2,1,0:T(8,128)S(1)}, f32[2,127,4]{2,1,0:T(8,128)}, u32[]{:S(2)}) copy-start(f32[2,127,4]{2,1,0:T(8,128)} %copy.122) | copy-start | bytes 12196
Sparse Core Ops, SparseCore 0:
  677.8 203.5 all-gather.10
  889.4 187.6 all-gather.12
